TPU v7x, 32 devices: a whole 2x2x4 slice. The times are simulated.
32 devices in a mesh: ell: 16 (over z, y, core), chan: 2 (over x).
Axes of the slice: x: 2, y: 2, z: 4, core: 2. Of those that a mesh axis runs over, the one named last changes fastest.
Arguments:
- sky_alm: bfloat16 [4, 1024, 24576], P('chan', 'ell'), may hold values from -6 to 6
- beam_transfer: bfloat16 [4, 16, 128, 16, 1536], P('chan', 'ell'), may hold values from -0.15625 to 0.15625
- slot_rows: int32 [16, 128], P('ell'), may hold values from 0 to 127, as said below
- block_count: int32 [16], P('ell'), may hold values from 1 to 128, as said below
Outputs:
- visibility: bfloat16 [4, 128, 16, 1024], P('chan', 'ell')
Inputs may be any that keep to these rules, and one draw needn't show every extreme that they name: `block_count`: every l-block has at least one live slot, and some l-block has exactly 128. `slot_rows`: the 128 entries of one l-block are distinct baselines; only the first block_count of them are live.
All inputs are finite; a program needn't handle non-finite values.
Results may differ from a plain program's by a relative error of at most 0.012.
Values may be sent and summed in bfloat16 or wider, within the bound.
A program may use at most 192 MiB of HBM per device.

v0:
```python
import jax
import jax.numpy as jnp
from jax import lax
from jax.sharding import PartitionSpec as P

BL_OWN = 8


def local(sky_alm, beam_transfer, slot_rows, block_count):
    local_sky = lax.all_to_all(sky_alm, "ell", split_axis=2, concat_axis=1, tiled=True)
    beam_rows = beam_transfer[:, 0]
    channels = beam_rows.shape[0]
    capacity = beam_rows.shape[1]
    components = beam_rows.shape[2]
    realizations = local_sky.shape[1]
    live_count = block_count[0]
    slot_number = jnp.arange(capacity, dtype=jnp.int32)
    partial_sums = jnp.einsum(
        "cpvk,crk->cpvr", beam_rows, local_sky, preferred_element_type=jnp.float32
    )
    inside = slot_number < live_count
    partial_sums = jnp.where(inside[None, :, None, None], partial_sums, 0.0)
    total_rows = BL_OWN * lax.axis_size("ell")
    dense_terms = jnp.zeros((channels, total_rows, components, realizations), jnp.float32)
    dense_terms = dense_terms.at[:, slot_rows[0]].add(partial_sums)
    owned = lax.psum_scatter(
        dense_terms.astype(jnp.bfloat16), "ell", scatter_dimension=1, tiled=True
    )
    return owned


def solution(mesh):
    in_specs = (
        P("chan", "ell", None),
        P("chan", "ell", None, None, None),
        P("ell", None),
        P("ell"),
    )
    out_specs = P("chan", "ell", None, None)
    return jax.shard_map(local, mesh=mesh, in_specs=in_specs, out_specs=out_specs, check_vma=False)
```

profile of v0, /device:TPU:0, one launch (start us, length us, event | category | flops | bytes accessed | tf_op | source)
XLA Modules:
  0.0 474.2 jit_solution(1491780624024285034)
XLA Ops:
  6.5 25.9 %copy.12 = bf16[2,64,24576]{1,0,2:T(2,128)(2,1)} copy(bf16[2,64,24576]{2,1,0:T(8,128)(2,1)} %param.4) | data formatting | bytes 12582912 | tf_op args[0]
  32.5 0.0 copy-start
  32.5 16.7 %reshape.43 = bf16[16,2,98304]{2,1,0:T(2,128)(2,1)} reshape(bf16[24576,2,64]{2,1,0:T(2,128)(2,1)} %bitcast.34) | data formatting | bytes 12582912
  49.1 7.5 %all-to-all-start = ((bf16[16,2,98304]{2,1,0:T(2,128)(2,1)}), bf16[16,2,98304]{2,1,0:T(2,128)(2,1)}, u32[]{:S(2)}, u32[]{:S(2)}) async-start(bf16[16,2,98304]{2,1,0:T(2,128)(2,1)} %reshape.43), calls=%async_computation | async-start | bytes 12582912 | tf_op jit(solution)/shard_map/all_to_all | solution.py:10
  56.6 0.0 reduce-scatter.5.cloned.1.call-start
  57.3 0.0 copy-done
  57.3 113.3 %all-to-all-done = bf16[16,2,98304]{2,1,0:T(2,128)(2,1)} async-done(((bf16[16,2,98304]{2,1,0:T(2,128)(2,1)}), bf16[16,2,98304]{2,1,0:T(2,128)(2,1)}, u32[]{:S(2)}, u32[]{:S(2)}) %all-to-all-start) | async-done | bytes 6291488 | tf_op jit(solution)/shard_map/all_to_all | solution.py:10
  170.7 16.3 %reshape.44 = bf16[24576,2,64]{2,1,0:T(2,128)(2,1)} reshape(bf16[16,2,98304]{2,1,0:T(2,128)(2,1)} %all-to-all-done) | data formatting | bytes 12582912
  187.0 29.7 %copy.13 = bf16[2,64,16,1536]{3,1,2,0:T(8,128)(2,1)} copy(bf16[2,64,16,1536]{1,0,3,2:T(2,128)(2,1)} %bitcast.33) | data formatting | bytes 12582912 | tf_op jit(solution)/shard_map/all_to_all | solution.py:10
  216.7 26.8 %select_bitcast_fusion = f32[128,2,16,1024]{3,0,2,1:T(8,128)} fusion(pred[128]{0:T(512)(128)(4,1)S(1)} %iota_compare_fusion, bf16[2,1024,1536,1]{2,1,3,0:T(8,128)(2,1)} %bitcast.37, bf16[2,128,16,1536]{3,2,1,0:T(8,128)(2,1)} %bitcast.39), kind=kOutput, calls=%fused_computation.1 | convolution fusion | flops 12889096192 | bytes 35651712 | tf_op jit(solution)/shard_map/cpvk,crk->cpvr/dot_general | solution.py:18
  243.5 17.7 %copy.16 = f32[128,2,16,1024]{3,2,1,0:T(8,128)} copy(f32[128,2,16,1024]{3,0,2,1:T(8,128)} %select_bitcast_fusion) | data formatting | bytes 33554432 | tf_op jit(solution)/shard_map/jit(_where)/select_n | solution.py:22
  261.2 7.9 %broadcast_in_dim.15.clone = f32[2,128,16,1024]{3,2,1,0:T(8,128)} broadcast(f32[]{:T(128)} %constant.3.clone.1), dimensions={} | broadcast | bytes 16777220 | tf_op jit(solution)/shard_map/broadcast_in_dim | solution.py:24
  269.0 39.0 %scatter_fusion = f32[2,128,16,1024]{3,2,1,0:T(8,128)} fusion(f32[2,128,16,1024]{3,2,1,0:T(8,128)} %broadcast_in_dim.15.clone, s32[128]{0:T(128)S(1)} %fusion.4, f32[128,2,16,1024]{3,2,1,0:T(8,128)} %copy.16), kind=kCustom, calls=%fused_computation | custom fusion | flops 4194304 | bytes 50332160 | tf_op jit(solution)/shard_map/scatter-add | solution.py:25
  308.0 9.1 %convert_element_type.3 = bf16[2,128,16,1024]{3,2,1,0:T(8,128)(2,1)} convert(f32[2,128,16,1024]{3,2,1,0:T(8,128)} %scatter_fusion) | non-fusion elementwise | flops 4194304 | bytes 25165824 | tf_op jit(solution)/shard_map/convert_element_type | solution.py:27
  317.1 8.5 %copy.18 = bf16[2,128,16,1024]{3,2,0,1:T(8,128)(2,1)} copy(bf16[2,128,16,1024]{3,2,1,0:T(8,128)(2,1)} %convert_element_type.3) | data formatting | bytes 16777216
  325.7 12.6 %copy.20 = bf16[16,8,32,1024]{3,1,2,0:T(8,128)(2,1)} copy(bf16[16,8,32,1024]{3,2,1,0:T(8,128)(2,1)} %bitcast.36) | data formatting | bytes 16777216
  338.3 0.0 reduce-scatter.5.cloned.1.call-update
  338.3 127.0 %reduce-scatter.5.cloned.1.call-done = bf16[8,32768]{1,0:T(8,128)(2,1)} async-done(((bf16[128,32768]{1,0:T(8,128)(2,1)}), bf16[8,32768]{1,0:T(8,128)(2,1)}) %reduce-scatter.5.cloned.1.call-update) | async-done | bytes 524304
  465.2 2.1 copy.19
  (2 shorter events, 0.0 us)
Async XLA Ops:
  32.5 24.8 %copy-start = (s32[1,128]{1,0:T(1,128)S(1)}, s32[1,128]{1,0:T(1,128)}, u32[]{:S(2)}) copy-start(s32[1,128]{1,0:T(1,128)} %param.6) | copy-start | bytes 1540
  49.1 121.5 %all-to-all-start = ((bf16[16,2,98304]{2,1,0:T(2,128)(2,1)}), bf16[16,2,98304]{2,1,0:T(2,128)(2,1)}, u32[]{:S(2)}, u32[]{:S(2)}) async-start(bf16[16,2,98304]{2,1,0:T(2,128)(2,1)} %reshape.43), calls=%async_computation | async-start | bytes 12582912 | tf_op jit(solution)/shard_map/all_to_all | solution.py:10
  56.6 408.6 %reduce-scatter.5.cloned.1.call-start = ((), (), s32[]{:S(2)}) async-start(), calls=%async_computation.2 | async-start | bytes 8912896
Sparse Core Ops, SparseCore 0:
  338.4 126.7 reduce-scatter.4
where the time goes:
time: 477 us; the launch traced here: 474 us
  waiting for transfers between devices  240 us (50%)
  local copies, waits for them, and re-layouts  137 us (29%)
  other arithmetic  48.1 us (10%)
  matrix products  26.8 us (6%)
  between operations  14.1 us (3%)
  starting transfers between devices  7.5 us (2%)
    unnamed x2, waiting for transfers between devices  127 us
    all_to_all x1, waiting for transfers between devices, local(): lax.all_to_all(sky_alm, 'ell', split_axis=2, concat_axis=1, tiled=True)  113 us
    unnamed x8, local copies, waits for them, and re-layouts  82.2 us
    scatter-add x1, other arithmetic, local(): dense_terms = dense_terms.at[:, slot_rows[0]].add(partial_sums)  39 us
    all_to_all x1, local copies, waits for them, and re-layouts, local(): lax.all_to_all(sky_alm, 'ell', split_axis=2, concat_axis=1, tiled=True)  29.7 us
    dot_general x1, matrix products, local(): jnp.einsum('cpvk,crk->cpvr', beam_rows, local_sky, preferred_element_type...  26.8 us
    select_n x1, local copies, waits for them, and re-layouts, local(): partial_sums = jnp.where(inside[None, :, None, None], partial_sums, 0.0)  17.7 us
  transfers between devices with their start and end apart: 2, of which 2 were waited for; matrix products, arithmetic and copies ran while one was open for 0% of the time, Pallas kernels for 0%

commit v1 on v0

v1 whole, which is shorter than its diff:
```python
import functools

import jax
import jax.numpy as jnp
from jax import lax
from jax.experimental import pallas as pl
from jax.experimental.pallas import tpu as pltpu
from jax.sharding import PartitionSpec as P

BL_OWN = 8
LOOKAHEAD = 2
STEP_ROWS = 16
GROUP = 4


def bit(value, at):
    return (value // (1 << at)) % 2


def kernel(n, levels, quarters, slot_ref, sky_ref, beam_ref, out_ref, beam_in, dense, held, part, got, place,
           beam_sem, own_sem, sky_send, sky_recv, sum_send, sum_recv):
    me = lax.axis_index("ell")
    channels, capacity, components = beam_in.shape[0], beam_in.shape[1] - 1, beam_in.shape[2]
    depth = beam_in.shape[3]
    phases = channels * quarters
    rows = STEP_ROWS
    width = n * rows

    def dest_of(position):
        total = 0
        for level in range(levels):
            flip = bit(position, levels - 1 - level)
            total = total + ((bit(me, level) + flip) % 2) * (1 << level)
        return total

    def partner_of(level):
        return me + (1 - 2 * bit(me, level)) * (1 << level)

    def sky_block(phase, owner):
        channel, quarter = phase // quarters, phase % quarters
        return sky_ref.at[
            channel,
            pl.ds(pl.multiple_of(quarter * rows, rows), rows),
            pl.ds(pl.multiple_of(owner * depth, 128), depth),
        ]

    def send_sky(phase):
        pltpu.make_async_copy(sky_block(phase, me), held.at[phase, me], own_sem.at[phase]).start()

        def one(k, carry):
            offset = n - 1 - k
            target = (me + offset) % n
            pltpu.make_async_remote_copy(
                src_ref=sky_block(phase, target),
                dst_ref=held.at[phase, me],
                send_sem=sky_send.at[phase],
                recv_sem=sky_recv.at[phase],
                device_id={"ell": target},
                device_id_type=pl.DeviceIdType.MESH,
            ).start()
            return carry

        lax.fori_loop(0, n - 1, one, 0)

    def others(phase, sem):
        block = held.at[phase, pl.ds(0, n - 1)]
        return pltpu.make_async_copy(block, block, sem.at[phase])

    def sum_copy(phase, level):
        size = n >> (level + 1)
        return pltpu.make_async_remote_copy(
            src_ref=part.at[phase, pl.ds(size, size)],
            dst_ref=got.at[phase, pl.ds(size - 1, size)],
            send_sem=sum_send.at[level, phase],
            recv_sem=sum_recv.at[level, phase],
            device_id={"ell": partner_of(level)},
            device_id_type=pl.DeviceIdType.MESH,
        )

    beam_copy = pltpu.make_async_copy(beam_ref.at[:, 0], beam_in.at[:, pl.ds(0, capacity)], beam_sem)
    beam_copy.start()

    barrier = pltpu.get_barrier_semaphore()

    def greet(k, carry):
        pl.semaphore_signal(
            barrier, inc=1, device_id={"ell": (me + 1 + k) % n}, device_id_type=pl.DeviceIdType.MESH
        )
        return carry

    lax.fori_loop(0, n - 1, greet, 0)
    pl.semaphore_wait(barrier, n - 1)

    for phase in range(min(LOOKAHEAD, phases)):
        send_sky(phase)

    for channel in range(channels):
        beam_in[channel, capacity] = jnp.zeros((components, depth), beam_in.dtype)
    local_rows = place.shape[1] // n

    def fill_place(quarter, carry):
        source = lax.broadcasted_iota(jnp.int32, (width, place.shape[1]), 0)
        column = lax.broadcasted_iota(jnp.int32, (width, place.shape[1]), 1)
        goal = (source // rows) * local_rows + source % rows + quarter * rows
        start = pl.multiple_of(quarter * width, width)
        place[pl.ds(start, width), :] = jnp.where(goal == column, 1.0, 0.0).astype(place.dtype)
        return carry

    lax.fori_loop(0, quarters, fill_place, 0)
    beam_copy.wait()

    def fill_dense(position, carry):
        base = dest_of(position) * BL_OWN
        for i in range(BL_OWN):
            slot = slot_ref[base + i]
            for channel in range(channels):
                dense[channel, position, i * components:(i + 1) * components, :] = beam_in[channel, slot]
        return carry

    lax.fori_loop(0, n, fill_dense, 0)

    def multiply(phase, first, count):
        channel = phase // quarters
        tile = dense.shape[2]

        def one(g, carry):
            at = first + g * GROUP
            left = dense[channel, pl.ds(at, GROUP)].reshape(GROUP * tile, depth)
            right = held[phase].reshape(width, depth)
            product = lax.dot_general(
                left, right, (((1,), (1,)), ((), ())), preferred_element_type=jnp.float32
            )
            part[phase, pl.ds(at, GROUP)] = product.reshape(GROUP, tile, width).astype(part.dtype)
            return carry

        lax.fori_loop(0, count // GROUP, one, 0)

    def add_level(phase, level):
        size = n >> (level + 1)
        sum_copy(phase, level).wait_recv()

        def one(q, carry):
            total = part[phase, q].astype(jnp.float32) + got[phase, q + size - 1].astype(jnp.float32)
            part[phase, q] = total.astype(part.dtype)
            return carry

        lax.fori_loop(0, size, one, 0)
        if level + 1 < levels:
            sum_copy(phase, level + 1).start()

    def step(t, carry):
        @pl.when(t + LOOKAHEAD < phases)
        def _():
            send_sky(t + LOOKAHEAD)

        for level in reversed(range(levels)):
            phase = t - 1 - level

            @pl.when((phase >= 0) & (phase < phases))
            def _():
                add_level(phase, level)

        @pl.when(t < phases)
        def _():
            pltpu.make_async_copy(sky_block(t, me), held.at[t, me], own_sem.at[t]).wait()
            others(t, sky_recv).wait()
            multiply(t, n // 2, n // 2)
            sum_copy(t, 0).start()
            multiply(t, 0, n // 2)

        return carry

    lax.fori_loop(0, phases + levels, step, 0)

    for channel in range(channels):
        total = jnp.zeros(out_ref.shape[1:], jnp.float32)
        for quarter in range(quarters):
            total = total + jnp.dot(
                part[channel * quarters + quarter, 0],
                place[quarter * width:(quarter + 1) * width, :],
                preferred_element_type=jnp.float32,
            )
        out_ref[channel] = total.astype(out_ref.dtype)

    def drain(phase, carry):
        others(phase, sky_send).wait()
        for level in range(levels):
            sum_copy(phase, level).wait_send()
        return carry

    lax.fori_loop(0, phases, drain, 0)


def local(n, sky_alm, beam_transfer, slot_rows, block_count):
    channels, local_rows = sky_alm.shape[:2]
    capacity, components, depth = beam_transfer.shape[2:]
    levels = n.bit_length() - 1
    quarters = local_rows // STEP_ROWS
    phases = channels * quarters
    width = n * STEP_ROWS
    tile = BL_OWN * components
    total_rows = BL_OWN * n
    slots = jnp.arange(capacity, dtype=jnp.int32)
    hit = (slot_rows[0][None, :] == jnp.arange(total_rows, dtype=jnp.int32)[:, None]) & (slots < block_count[0])[None, :]
    slot_of_row = jnp.min(jnp.where(hit, slots[None, :], capacity), axis=1)
    out = pl.pallas_call(
        functools.partial(kernel, n, levels, quarters),
        out_shape=jax.ShapeDtypeStruct((channels, tile, n * local_rows), jnp.bfloat16),
        in_specs=[
            pl.BlockSpec(memory_space=pltpu.SMEM),
            pl.BlockSpec(memory_space=pl.ANY),
            pl.BlockSpec(memory_space=pl.ANY),
        ],
        out_specs=pl.BlockSpec(memory_space=pltpu.VMEM),
        scratch_shapes=[
            pltpu.VMEM((channels, capacity + 1, components, depth), jnp.bfloat16),
            pltpu.VMEM((channels, n, tile, depth), jnp.bfloat16),
            pltpu.VMEM((phases, n, STEP_ROWS, depth), jnp.bfloat16),
            pltpu.VMEM((phases, n, tile, width), jnp.bfloat16),
            pltpu.VMEM((phases, n - 1, tile, width), jnp.bfloat16),
            pltpu.VMEM((quarters * width, n * local_rows), jnp.bfloat16),
            pltpu.SemaphoreType.DMA,
            pltpu.SemaphoreType.DMA((phases,)),
            pltpu.SemaphoreType.DMA((phases,)),
            pltpu.SemaphoreType.DMA((phases,)),
            pltpu.SemaphoreType.DMA((levels, phases)),
            pltpu.SemaphoreType.DMA((levels, phases)),
        ],
        compiler_params=pltpu.CompilerParams(
            collective_id=0, has_side_effects=True, vmem_limit_bytes=67043328
        ),
    )(slot_of_row, sky_alm, beam_transfer)
    return out.reshape(channels, BL_OWN, components, n * local_rows)


def solution(mesh):
    in_specs = (
        P("chan", "ell", None),
        P("chan", "ell", None, None, None),
        P("ell", None),
        P("ell"),
    )
    out_specs = P("chan", "ell", None, None)
    return jax.shard_map(
        functools.partial(local, mesh.shape["ell"]),
        mesh=mesh,
        in_specs=in_specs,
        out_specs=out_specs,
        check_vma=False,
    )
```

time: 477 us -> 187 us (0.39)
  waiting for transfers between devices: 240 us -> 0 us
  Pallas kernels: 0 us -> 183 us
  local copies, waits for them, and re-layouts: 137 us -> 1.88 us
  other arithmetic: 48.1 us -> 1.29 us
  matrix products: 26.8 us -> 0 us
  between operations: 14.1 us -> 0.67 us
  starting transfers between devices: 7.5 us -> 0 us
    pallas_call x0 -> x1, Pallas kernels: none -> 183 us  [local(): pl.pallas_call(functools.partial(kernel, n, levels, quarters), out_shape=...]
    unnamed x2 -> x0, waiting for transfers between devices: 127 us -> none
    all_to_all x1 -> x0, waiting for transfers between devices: 113 us -> none  [local(): lax.all_to_all(sky_alm, 'ell', split_axis=2, concat_axis=1, tiled=True)]
    unnamed x8 -> x1, local copies, waits for them, and re-layouts: 82.2 us -> 1.88 us
    scatter-add x1 -> x0, other arithmetic: 39 us -> none  [local(): dense_terms = dense_terms.at[:, slot_rows[0]].add(partial_sums)]
    all_to_all x1 -> x0, local copies, waits for them, and re-layouts: 29.7 us -> none  [local(): lax.all_to_all(sky_alm, 'ell', split_axis=2, concat_axis=1, tiled=True)]
    dot_general x1 -> x0, matrix products: 26.8 us -> none  [local(): jnp.einsum('cpvk,crk->cpvr', beam_rows, local_sky, preferred_element_type...]
    select_n x1 -> x0, local copies, waits for them, and re-layouts: 17.7 us -> none  [local(): partial_sums = jnp.where(inside[None, :, None, None], partial_sums, 0.0)]
  transfers between devices with their start and end apart: 2 -> 0, of which waited for: 2 -> 0; matrix products, arithmetic and copies ran while one was open for 0% -> 0% of each run, Pallas kernels for 0% -> 0%
where the time goes in v1:
time: 187 us; the launch traced here: 186 us
  Pallas kernels  183 us (98%)
  local copies, waits for them, and re-layouts  1.88 us (1%)
    pallas_call x1, Pallas kernels, local(): pl.pallas_call(functools.partial(kernel, n, levels, quarters), out_shape=...  183 us

profile of v1, /device:TPU:0, one launch (start us, length us, event | category | flops | bytes accessed | tf_op | source)
XLA Modules:
  0.0 186.4 jit_solution(18177277158717804232)
XLA Ops:
  0.7 1.3 select_reduce_fusion.slot_ref
  1.9 182.6 %shard_map.46 = bf16[2,128,1024]{2,1,0:T(8,128)(2,1)} custom-call(s32[128]{0:T(128)} %select_reduce_fusion.slot_ref, bf16[2,64,24576]{2,1,0:T(8,128)(2,1)} %sky_ref.1, bf16[2,1,128,16,1536]{4,3,2,1,0:T(8,128)(2,1)} %beam_ref.1), custom_call_target="tpu_custom_call" | custom-call | tf_op jit(solution)/shard_map/pallas_call | solution.py:206
  184.6 1.9 %copy.7 = bf16[2,8,16,1024]{3,2,1,0:T(8,128)(2,1)} copy(bf16[2,8,16,1024]{3,2,1,0:T(8,128)(2,1)} %bitcast.4) | data formatting | bytes 1048576
  (1 shorter events, 0.0 us)

commit v2 on v1

--- a/solution.py
+++ b/solution.py
@@ -8,7 +8,7 @@
 from jax.sharding import PartitionSpec as P
 
 BL_OWN = 8
-LOOKAHEAD = 2
+LOOKAHEAD = 1
 STEP_ROWS = 16
 GROUP = 4
 
@@ -17,12 +17,13 @@
     return (value // (1 << at)) % 2
 
 
-def kernel(n, levels, quarters, slot_ref, sky_ref, beam_ref, out_ref, beam_in, dense, held, part, got, place,
-           beam_sem, own_sem, sky_send, sky_recv, sum_send, sum_recv):
+def kernel(n, levels, quarters, rows_ref, count_ref, sky_ref, beam_ref, out_ref, slot_vec, slot_ref, beam_in, dense, held, part, got, place,
+           slot_sem, beam_sem, own_sem, sky_send, sky_recv, sum_send, sum_recv):
     me = lax.axis_index("ell")
     channels, capacity, components = beam_in.shape[0], beam_in.shape[1] - 1, beam_in.shape[2]
     depth = beam_in.shape[3]
     phases = channels * quarters
+    release = phases - 2
     rows = STEP_ROWS
     width = n * rows
 
@@ -48,8 +49,7 @@
         pltpu.make_async_copy(sky_block(phase, me), held.at[phase, me], own_sem.at[phase]).start()
 
         def one(k, carry):
-            offset = n - 1 - k
-            target = (me + offset) % n
+            target = (me + n - 1 - k) % n
             pltpu.make_async_remote_copy(
                 src_ref=sky_block(phase, target),
                 dst_ref=held.at[phase, me],
@@ -94,6 +94,14 @@
     for phase in range(min(LOOKAHEAD, phases)):
         send_sky(phase)
 
+    shape = (capacity, n * BL_OWN)
+    slots = lax.broadcasted_iota(jnp.int32, shape, 0)
+    held_rows = jnp.broadcast_to(rows_ref[...], shape[::-1]).T
+    hit = (held_rows == lax.broadcasted_iota(jnp.int32, shape, 1)) & (slots < count_ref[0])
+    slot_vec[...] = jnp.min(jnp.where(hit, slots, capacity), axis=0, keepdims=True)
+    slot_copy = pltpu.make_async_copy(slot_vec, slot_ref, slot_sem)
+    slot_copy.start()
+
     for channel in range(channels):
         beam_in[channel, capacity] = jnp.zeros((components, depth), beam_in.dtype)
     local_rows = place.shape[1] // n
@@ -107,12 +115,13 @@
         return carry
 
     lax.fori_loop(0, quarters, fill_place, 0)
+    slot_copy.wait()
     beam_copy.wait()
 
     def fill_dense(position, carry):
         base = dest_of(position) * BL_OWN
         for i in range(BL_OWN):
-            slot = slot_ref[base + i]
+            slot = slot_ref[0, base + i]
             for channel in range(channels):
                 dense[channel, position, i * components:(i + 1) * components, :] = beam_in[channel, slot]
         return carry
@@ -135,7 +144,7 @@
 
         lax.fori_loop(0, count // GROUP, one, 0)
 
-    def add_level(phase, level):
+    def add_level(phase, level, send):
         size = n >> (level + 1)
         sum_copy(phase, level).wait_recv()
 
@@ -145,20 +154,30 @@
             return carry
 
         lax.fori_loop(0, size, one, 0)
-        if level + 1 < levels:
-            sum_copy(phase, level + 1).start()
+
+        @pl.when(send)
+        def _():
+            sum_copy(phase, min(level + 1, levels - 1)).start()
 
     def step(t, carry):
         @pl.when(t + LOOKAHEAD < phases)
         def _():
             send_sky(t + LOOKAHEAD)
 
-        for level in reversed(range(levels)):
+        for level in range(levels - 1):
             phase = t - 1 - level
 
             @pl.when((phase >= 0) & (phase < phases))
             def _():
-                add_level(phase, level)
+                add_level(phase, level, t >= release if level == levels - 2 else t >= 0)
+
+        @pl.when(t == release)
+        def _():
+            def one(phase, inner):
+                sum_copy(phase, levels - 1).start()
+                return inner
+
+            lax.fori_loop(0, release - levels + 1, one, 0)
 
         @pl.when(t < phases)
         def _():
@@ -170,7 +189,13 @@
 
         return carry
 
-    lax.fori_loop(0, phases + levels, step, 0)
+    lax.fori_loop(0, phases + levels - 1, step, 0)
+
+    def finish(phase, carry):
+        add_level(phase, levels - 1, phase < 0)
+        return carry
+
+    lax.fori_loop(0, phases, finish, 0)
 
     for channel in range(channels):
         total = jnp.zeros(out_ref.shape[1:], jnp.float32)
@@ -199,26 +224,26 @@
     phases = channels * quarters
     width = n * STEP_ROWS
     tile = BL_OWN * components
-    total_rows = BL_OWN * n
-    slots = jnp.arange(capacity, dtype=jnp.int32)
-    hit = (slot_rows[0][None, :] == jnp.arange(total_rows, dtype=jnp.int32)[:, None]) & (slots < block_count[0])[None, :]
-    slot_of_row = jnp.min(jnp.where(hit, slots[None, :], capacity), axis=1)
     out = pl.pallas_call(
         functools.partial(kernel, n, levels, quarters),
         out_shape=jax.ShapeDtypeStruct((channels, tile, n * local_rows), jnp.bfloat16),
         in_specs=[
+            pl.BlockSpec(memory_space=pltpu.VMEM),
             pl.BlockSpec(memory_space=pltpu.SMEM),
             pl.BlockSpec(memory_space=pl.ANY),
             pl.BlockSpec(memory_space=pl.ANY),
         ],
         out_specs=pl.BlockSpec(memory_space=pltpu.VMEM),
         scratch_shapes=[
+            pltpu.VMEM((1, n * BL_OWN), jnp.int32),
+            pltpu.SMEM((1, n * BL_OWN), jnp.int32),
             pltpu.VMEM((channels, capacity + 1, components, depth), jnp.bfloat16),
             pltpu.VMEM((channels, n, tile, depth), jnp.bfloat16),
             pltpu.VMEM((phases, n, STEP_ROWS, depth), jnp.bfloat16),
             pltpu.VMEM((phases, n, tile, width), jnp.bfloat16),
             pltpu.VMEM((phases, n - 1, tile, width), jnp.bfloat16),
             pltpu.VMEM((quarters * width, n * local_rows), jnp.bfloat16),
+            pltpu.SemaphoreType.DMA,
             pltpu.SemaphoreType.DMA,
             pltpu.SemaphoreType.DMA((phases,)),
             pltpu.SemaphoreType.DMA((phases,)),
@@ -229,7 +254,7 @@
         compiler_params=pltpu.CompilerParams(
             collective_id=0, has_side_effects=True, vmem_limit_bytes=67043328
         ),
-    )(slot_of_row, sky_alm, beam_transfer)
+    )(slot_rows, block_count, sky_alm, beam_transfer)
     return out.reshape(channels, BL_OWN, components, n * local_rows)
 
 

time: 187 us -> 175 us (0.936)
  Pallas kernels: 183 us -> 172 us
    pallas_call x1, Pallas kernels: 183 us -> 172 us  [local(): pl.pallas_call(functools.partial(kernel, n, levels, quarters), out_shape=...]
where the time goes in v2:
time: 175 us; the launch traced here: 174 us
  Pallas kernels  172 us (98%)
  local copies, waits for them, and re-layouts  1.88 us (1%)
    pallas_call x1, Pallas kernels, local(): pl.pallas_call(functools.partial(kernel, n, levels, quarters), out_shape=...  172 us

profile of v2, /device:TPU:0, one launch (start us, length us, event | category | flops | bytes accessed | tf_op | source)
XLA Modules:
  0.0 174.2 jit_solution(8203411018849024739)
XLA Ops:
  0.7 171.7 %shard_map.46 = bf16[2,128,1024]{2,1,0:T(8,128)(2,1)} custom-call(s32[1,128]{1,0:T(1,128)} %rows_ref.1, s32[1]{0:T(128)S(6)} %copy.6.count_ref, bf16[2,64,24576]{2,1,0:T(8,128)(2,1)} %sky_ref.1, bf16[2,1,128,16,1536]{4,3,2,1,0:T(8,128)(2,1)} %beam_ref.1), custom_call_target="tpu_custom_call" | custom-call | tf_op jit(solution)/shard_map/pallas_call | solution.py:227
  172.3 1.9 %copy.7 = bf16[2,8,16,1024]{3,2,1,0:T(8,128)(2,1)} copy(bf16[2,8,16,1024]{3,2,1,0:T(8,128)(2,1)} %bitcast.1) | data formatting | bytes 1048576

commit v3 on v2

--- a/solution.py
+++ b/solution.py
@@ -17,7 +17,7 @@
     return (value // (1 << at)) % 2
 
 
-def kernel(n, levels, quarters, rows_ref, count_ref, sky_ref, beam_ref, out_ref, slot_vec, slot_ref, beam_in, dense, held, part, got, place,
+def kernel(n, levels, quarters, rows_ref, count_ref, sky_ref, beam_ref, out_ref, slot_vec, slot_ref, beam_in, dense, held, part, got, place, gathered,
            slot_sem, beam_sem, own_sem, sky_send, sky_recv, sum_send, sum_recv):
     me = lax.axis_index("ell")
     channels, capacity, components = beam_in.shape[0], beam_in.shape[1] - 1, beam_in.shape[2]
@@ -195,17 +195,25 @@
         add_level(phase, levels - 1, phase < 0)
         return carry
 
-    lax.fori_loop(0, phases, finish, 0)
-
+    def placed(phase):
+        quarter = phase % quarters
+        return jnp.dot(
+            part[phase, 0], place[quarter * width:(quarter + 1) * width, :], preferred_element_type=jnp.float32
+        )
+
+    lax.fori_loop(0, phases - 1, finish, 0)
     for channel in range(channels):
+        first = channel * quarters
+        last = first + quarters
         total = jnp.zeros(out_ref.shape[1:], jnp.float32)
-        for quarter in range(quarters):
-            total = total + jnp.dot(
-                part[channel * quarters + quarter, 0],
-                place[quarter * width:(quarter + 1) * width, :],
-                preferred_element_type=jnp.float32,
-            )
-        out_ref[channel] = total.astype(out_ref.dtype)
+        for phase in range(first, min(last, phases - 1)):
+            total = total + placed(phase)
+        if last == phases:
+            gathered[...] = total
+        else:
+            out_ref[channel] = total.astype(out_ref.dtype)
+    finish(phases - 1, 0)
+    out_ref[channels - 1] = (gathered[...] + placed(phases - 1)).astype(out_ref.dtype)
 
     def drain(phase, carry):
         others(phase, sky_send).wait()
@@ -243,6 +251,7 @@
             pltpu.VMEM((phases, n, tile, width), jnp.bfloat16),
             pltpu.VMEM((phases, n - 1, tile, width), jnp.bfloat16),
             pltpu.VMEM((quarters * width, n * local_rows), jnp.bfloat16),
+            pltpu.VMEM((tile, n * local_rows), jnp.float32),
             pltpu.SemaphoreType.DMA,
             pltpu.SemaphoreType.DMA,
             pltpu.SemaphoreType.DMA((phases,)),

time: 175 us -> 174 us (level)
  no operation moved by 1% of the time
where the time goes in v3:
time: 174 us
  Pallas kernels  172 us (99%)
  local copies, waits for them, and re-layouts  1.88 us (1%)
    pallas_call x1, Pallas kernels, local(): pl.pallas_call(functools.partial(kernel, n, levels, quarters), out_shape=...  172 us

profile of v3, /device:TPU:0, one launch (start us, length us, event | category | flops | bytes accessed | tf_op | source)
XLA Modules:
  0.0 174.2 jit_solution(8330798118211570788)
XLA Ops:
  0.7 171.7 %shard_map.46 = bf16[2,128,1024]{2,1,0:T(8,128)(2,1)} custom-call(s32[1,128]{1,0:T(1,128)} %rows_ref.1, s32[1]{0:T(128)S(6)} %copy.6.count_ref, bf16[2,64,24576]{2,1,0:T(8,128)(2,1)} %sky_ref.1, bf16[2,1,128,16,1536]{4,3,2,1,0:T(8,128)(2,1)} %beam_ref.1), custom_call_target="tpu_custom_call" | custom-call | tf_op jit(solution)/shard_map/pallas_call | solution.py:235
  172.3 1.9 %copy.7 = bf16[2,8,16,1024]{3,2,1,0:T(8,128)(2,1)} copy(bf16[2,8,16,1024]{3,2,1,0:T(8,128)(2,1)} %bitcast.1) | data formatting | bytes 1048576
